TPU v7x, 32 devices: a whole 2x2x4 slice. The times are simulated.
32 devices in a mesh: epoch: 4 (over z), vel: 8 (over y, x, core).
Axes of the slice: x: 2, y: 2, z: 4, core: 2. Of those that a mesh axis runs over, the one named last changes fastest.
Arguments:
- science: float32 [8, 32, 1024], P('epoch', 'vel'), may hold values from -6 to 6
- variance: float32 [8, 32, 1024], P('epoch', 'vel'), may hold values from 0.25 to 4
- psf: float32 [8, 9], P('epoch'), may hold values from 0.05 to 1
- shifts: int32 [2, 8, 8], P(None, None, 'vel'), may hold values from -16 to 16, as said below
Outputs:
- likelihood: float32 [8, 32, 1024], P('vel', 'epoch')
Inputs may be any that keep to these rules, and one draw needn't show every extreme that they name: For each velocity, the shifts of epoch e are the floor of the velocity's integer rates times the epoch's time over the span of the times; the first epoch's shifts are zero, and times rise with the epoch.
All inputs are finite; a program needn't handle non-finite values.
Results may differ from a plain program's by a relative error of at most 0.0003.
Values sent between devices are 32-bit elements; how exact they have to be, the bound alone decides.
No kernel may reach another device: no remote copies, remote signals or barrier semaphores. Data moves between devices by JAX's collectives and lax.ppermute only.
A program may use at most 64 MiB of HBM per device.

v0:
```python
import jax
import jax.numpy as jnp
from jax import lax
from jax.sharding import PartitionSpec as P

MAXS = 16


def extended(block, sides, width):
    for axis, dim in sides:
        count = lax.axis_size(axis)
        forward = [(i, i + 1) for i in range(count - 1)]
        backward = [(target, source) for source, target in forward]
        low = lax.ppermute(
            lax.slice_in_dim(block, block.shape[dim] - width, None, axis=dim), axis, forward
        )
        high = lax.ppermute(lax.slice_in_dim(block, 0, width, axis=dim), axis, backward)
        block = jnp.concatenate([low, block, high], axis=dim)
    return block


def filter_columns(pairing, weights):
    radius = weights.shape[2] // 2
    breadth = pairing.shape[3]
    padded = jnp.pad(pairing, ((0, 0), (0, 0), (0, 0), (radius, radius)))
    summed = jnp.zeros_like(pairing)
    for offset in range(weights.shape[2]):
        summed = (
            summed + weights[:, :, offset, None, None] * padded[:, :, :, offset : offset + breadth]
        )
    return summed


def filter_rows(rimmed, weights, height):
    summed = jnp.zeros(rimmed.shape[:2] + (height, rimmed.shape[3]), jnp.float32)
    for offset in range(weights.shape[2]):
        summed = (
            summed + weights[:, :, offset, None, None] * rimmed[:, :, offset : offset + height, :]
        )
    return summed


def per_device(science, variance, psf, shifts):
    slots = science.shape[0]
    height = science.shape[1]
    breadth = science.shape[2]
    radius = psf.shape[1] // 2
    pairing = jnp.stack([science / variance, 1.0 / variance], axis=1)
    weights = jnp.stack([psf, psf * psf], axis=1)
    columns_pass = filter_columns(pairing, weights)
    rimmed = extended(columns_pass, (("vel", 2),), radius)
    filtered = filter_rows(rimmed, weights, height)
    local_shifts = lax.dynamic_slice_in_dim(shifts, lax.axis_index("epoch") * slots, slots, 1)
    velocities = shifts.shape[2]
    gathered = lax.all_gather(filtered, "vel", axis=2, tiled=True)
    rows_all = gathered.shape[2]
    padded = jnp.pad(gathered, ((0, 0), (0, 0), (MAXS, MAXS), (MAXS, MAXS)))
    stacks = jnp.zeros((velocities, 2, rows_all, breadth), jnp.float32)
    for epoch_slot in range(slots):
        image = padded[epoch_slot]

        def window_at(shift_col, shift_row):
            return lax.dynamic_slice(
                image, (jnp.int32(0), MAXS + shift_row, MAXS + shift_col), (2, rows_all, breadth)
            )

        stacks = stacks + jax.vmap(window_at)(
            local_shifts[0, epoch_slot], local_shifts[1, epoch_slot]
        )
    mine = lax.psum_scatter(stacks, "epoch", scatter_dimension=2, tiled=True)
    return mine[:, 0] / jnp.sqrt(mine[:, 1])


def solution(mesh):
    return jax.shard_map(
        per_device,
        mesh=mesh,
        in_specs=(
            P("epoch", "vel", None),
            P("epoch", "vel", None),
            P("epoch", None),
            P(None, None, "vel"),
        ),
        out_specs=P("vel", "epoch", None),
        check_vma=False,
    )
```

profile of v0, /device:TPU:0, one launch (start us, length us, event | category | flops | bytes accessed | tf_op | source)
XLA Modules:
  0.0 81.5 jit_solution(1506419152563569825)
XLA Ops:
  6.5 0.0 all-reduce.5.cloned.1.call-start
  6.5 0.7 multiply_bitcast_fusion
  7.2 1.1 %fusion.26 = (f32[2,2,1]{2,0,1:T(2,128)S(1)}, f32[2,2,1]{2,0,1:T(2,128)S(1)}, f32[2,2,1]{2,0,1:T(2,128)S(1)}, f32[2,2,1]{2,0,1:T(2,128)S(1)}, f32[2,2,1]{2,0,1:T...) fusion(f32[2,1,9]{2,0,1:T(2,128)} %bitcast.58, ...), kind=kLoop, calls=%fused_computation.63 | loop fusion | flops 36 | bytes 288 | tf_op jit(solution)/shard_map/stack | solution.py:49
  8.3 0.1 copy.63
  8.4 0.1 copy.64
  8.5 0.1 copy.65
  8.6 0.1 copy.66
  8.7 0.1 copy.67
  8.8 0.1 copy.68
  8.9 0.1 copy.60
  9.0 0.1 copy.61
  9.1 0.1 copy.62
  9.2 0.8 divide_bitcast_fusion.1
  10.0 0.4 multiply_add_fusion
  10.4 2.4 %collective-permute-start = (f32[2,2,4,1024]{3,2,0,1:T(4,128)S(1)}, f32[2,2,4,1024]{3,2,0,1:T(4,128)S(1)}, u32[]{:S(2)}, u32[]{:S(2)}) collective-permute-start(f32[2,2,4,1024]{3,2,0,1:T(4,128)S(1)} %multiply_add_fusion), channel_id=1, source_target_pairs={{0,1},{1,2},{2,3},{3,4},{4,5},{5,6},{6,7},{8,9},{9,10},{10,11},{11... | collective-permute-start | bytes 196616 | tf_op jit(solution)/shard_map/ppermute | solution.py:14
  12.8 1.3 %collective-permute-start.1 = (f32[2,2,4,1024]{3,2,0,1:T(4,128)S(1)}, f32[2,2,4,1024]{3,2,0,1:T(4,128)S(1)}, u32[]{:S(2)}, u32[]{:S(2)}) collective-permute-start(f32[2,2,4,1024]{3,2,0,1:T(4,128)S(1)} %multiply_add_fusion), channel_id=1, source_target_pairs={{1,0},{2,1},{3,2},{4,3},{5,4},{6,5},{7,6},{9,8},{10,9},{11,10},{12... | collective-permute-start | bytes 196616 | tf_op jit(solution)/shard_map/ppermute | solution.py:17
  14.1 1.4 %constant_dynamic-slice_fusion = (s32[1,1,1]{1,2,0:T(1,128)}, s32[1,1,1]{1,2,0:T(1,128)}, s32[1,1,1]{1,2,0:T(1,128)}, s32[1,1,1]{1,2,0:T(1,128)}) fusion(s32[2,8,1]{1,2,0:T(1,128)} %param.7, s32[]{:T(128)S(6)} %select_n.15, s32[]{:T(128)S(6)} %add.166, s32[]{:T(128)S(6)} %add.168), kind=kLoop, calls=%fused_computation.71 | loop fusion | bytes 44 | tf_op jit(solution)/shard_map/slice | solution.py:68
  20.4 0.0 collective-permute-done
  20.5 0.0 collective-permute-done.1
  20.5 0.3 fusion.4
  20.7 0.1 copy.58
  20.8 14.1 %all_gather.3 = f32[2,2,32,1024]{3,1,0,2:T(2,128)S(1)} all-gather(f32[2,2,4,1024]{3,1,0,2:T(2,128)S(1)} %copy.58), channel_id=1, replica_groups=mesh['epoch'=4,'vel'=8] {'vel'}, dimensions={2}, use_global_device_ids=true | all-gather | bytes 589824 | tf_op jit(solution)/shard_map/all_gather | solution.py:55
  34.9 0.7 pad_slice_fusion.1
  35.6 0.0 copy-start
  35.7 1.3 %dynamic-slice_add_fusion = f32[1,2,32,1024]{3,1,0,2:T(2,128)} fusion(f32[1,2,64,1056]{3,1,0,2:T(2,128)S(1)} %get-tuple-element.28, s32[]{:T(128)} %bitcast.30, s32[]{:T(128)} %bitcast.33, f32[1,2,64,1056]{3,1,0,2:T(2,128)S(1)} %get-tuple-element.27, s32[]{:T(128)} %bitcast.24, s32[]{:T(128)} %bitcast.27), kind=kLoop, calls=%fused_computation.2 | loop fusion | flops 65536 | bytes 786448 | tf_op jit(solution)/shard_map/add | solution.py:67
  37.0 0.0 all-reduce.5.cloned.1.call-update
  37.0 0.0 copy-done
  37.0 0.6 dynamic-slice.10
  38.3 34.8 %all-reduce.5.cloned.1.call-done = f32[1,2,32,1024]{3,1,0,2:T(2,128)} async-done(((f32[1,2,32,1024]{3,1,0,2:T(2,128)}), f32[1,2,32,1024]{3,1,0,2:T(2,128)}) %all-reduce.5.cloned.1.call-update) | async-done | bytes 262160
  73.0 1.0 %fusion.24 = f32[1,8,1024]{2,0,1:T(1,128)S(1)} fusion(f32[1,2,32,1024]{3,1,0,2:T(2,128)} %all-reduce.5.cloned.1.call-done, u32[]{:T(128)S(6)} %convert, u32[]{:T(128)S(6)} %multiply.11), kind=kLoop, calls=%fused_computation.45 | loop fusion | flops 8192 | bytes 98312 | tf_op jit(solution)/shard_map/div | solution.py:71
  74.0 0.6 copy.59
  (1 shorter events, 0.0 us)
Async XLA Ops:
  6.5 66.5 %all-reduce.5.cloned.1.call-start = ((), (), s32[]{:S(2)}) async-start(), calls=%async_computation | async-start | bytes 524288
  10.4 10.0 %collective-permute-start = (f32[2,2,4,1024]{3,2,0,1:T(4,128)S(1)}, f32[2,2,4,1024]{3,2,0,1:T(4,128)S(1)}, u32[]{:S(2)}, u32[]{:S(2)}) collective-permute-start(f32[2,2,4,1024]{3,2,0,1:T(4,128)S(1)} %multiply_add_fusion), channel_id=1, source_target_pairs={{0,1},{1,2},{2,3},{3,4},{4,5},{5,6},{6,7},{8,9},{9,10},{10,11},{11... | collective-permute-start | bytes 196616 | tf_op jit(solution)/shard_map/ppermute | solution.py:14
  12.8 7.6 %collective-permute-start.1 = (f32[2,2,4,1024]{3,2,0,1:T(4,128)S(1)}, f32[2,2,4,1024]{3,2,0,1:T(4,128)S(1)}, u32[]{:S(2)}, u32[]{:S(2)}) collective-permute-start(f32[2,2,4,1024]{3,2,0,1:T(4,128)S(1)} %multiply_add_fusion), channel_id=1, source_target_pairs={{1,0},{2,1},{3,2},{4,3},{5,4},{6,5},{7,6},{9,8},{10,9},{11,10},{12... | collective-permute-start | bytes 196616 | tf_op jit(solution)/shard_map/ppermute | solution.py:17
  35.6 1.4 %copy-start = (u32[32]{0:T(128)S(1)}, u32[32]{0:T(128)}, u32[]{:S(2)}) copy-start(u32[32]{0:T(128)} %constant.89) | copy-start | bytes 388
Sparse Core Ops, SparseCore 0:
  37.1 35.8 all-reduce.4
where the time goes:
time: 81.9 us; the launch traced here: 81.5 us
  waiting for transfers between devices  34.8 us (42%)
  between operations  19.1 us (23%)
  blocking collectives  14.1 us (17%)
  other arithmetic  5.5 us (7%)
  local copies, waits for them, and re-layouts  4.27 us (5%)
  starting transfers between devices  3.69 us (5%)
    unnamed x2, waiting for transfers between devices  34.8 us
    all_gather x1, blocking collectives, per_device(): gathered = lax.all_gather(filtered, 'vel', axis=2, tiled=True)  14.1 us
    ppermute x1, starting transfers between devices, extended(): lax.ppermute(lax.slice_in_dim(block, block.shape[dim] - width, None, axis...  2.4 us
    another operation x2, other arithmetic, per_device(): weights = jnp.stack([psf, psf * psf], axis=1)  1.77 us
  transfers between devices with their start and end apart: 3, of which 1 were waited for; matrix products, arithmetic and copies ran while one was open for 2% of the time, Pallas kernels for 0%

commit v1 on v0

--- a/solution.py
+++ b/solution.py
@@ -52,7 +52,25 @@
     filtered = filter_rows(rimmed, weights, height)
     local_shifts = lax.dynamic_slice_in_dim(shifts, lax.axis_index("epoch") * slots, slots, 1)
     velocities = shifts.shape[2]
-    gathered = lax.all_gather(filtered, "vel", axis=2, tiled=True)
+    size, index, extent = (lax.axis_size("vel"), lax.axis_index("vel"), filtered.shape[2])
+    upward = [(i_2, (i_2 + 1) % size) for i_2 in range(size)]
+    left = [(i_2, (i_2 - 1) % size) for i_2 in range(size)]
+    gathered = jnp.zeros(
+        (*filtered.shape[:2], size * extent, *filtered.shape[2 + 1 :]), filtered.dtype
+    )
+    gathered = lax.dynamic_update_slice_in_dim(gathered, filtered, index * extent, axis=2)
+    from_left = from_right = filtered
+    middle = size // 2
+    for step in range(1, middle + 1):
+        from_left = lax.ppermute(from_left, "vel", upward)
+        gathered = lax.dynamic_update_slice_in_dim(
+            gathered, from_left, (index - step) % size * extent, axis=2
+        )
+        if step < size - middle:
+            from_right = lax.ppermute(from_right, "vel", left)
+            gathered = lax.dynamic_update_slice_in_dim(
+                gathered, from_right, (index + step) % size * extent, axis=2
+            )
     rows_all = gathered.shape[2]
     padded = jnp.pad(gathered, ((0, 0), (0, 0), (MAXS, MAXS), (MAXS, MAXS)))
     stacks = jnp.zeros((velocities, 2, rows_all, breadth), jnp.float32)

time: 81.9 us -> 73.7 us (0.90)
  blocking collectives: 14.1 us -> 0 us
  starting transfers between devices: 3.69 us -> 12 us
  local copies, waits for them, and re-layouts: 4.27 us -> 1.97 us
    unnamed x2 -> x1, waiting for transfers between devices: 34.8 us -> 0.02 us
    reduce_scatter x0 -> x1, waiting for transfers between devices: none -> 22.9 us  [per_device(): mine = lax.psum_scatter(stacks, 'epoch', scatter_dimension=2, tiled=True)]
    all_gather x1 -> x0, blocking collectives: 14.1 us -> none  [per_device(): gathered = lax.all_gather(filtered, 'vel', axis=2, tiled=True)]
    ppermute x0 -> x7, starting transfers between devices: none -> 8.33 us  [the longest x3 4.78 us: per_device(): from_right = lax.ppermute(from_right, 'vel', left)]
    ppermute x0 -> x7, waiting for transfers between devices: none -> 8.31 us  [the longest x4 8.3 us: per_device(): from_left = lax.ppermute(from_left, 'vel', upward)]
    ppermute x1, waiting for transfers between devices: 0.01 us -> 3.93 us  [extended(): lax.ppermute(lax.slice_in_dim(block, 0, width, axis=dim), axis, backward)]
    slice x0 -> x9, local copies, waits for them, and re-layouts: none -> 0.88 us  [the longest x8 0.78 us: filter_columns(): weights[:, :, offset, None, None] * padded[:, :, :, offset:offset + breadth]]
    mul x9 -> x0, local copies, waits for them, and re-layouts: 0.88 us -> none  [the longest x8 0.78 us: filter_columns(): weights[:, :, offset, None, None] * padded[:, :, :, offset:offset + breadth]]
  transfers between devices with their start and end apart: 3 -> 10, of which waited for: 1 -> 5; matrix products, arithmetic and copies ran while one was open for 2% -> 1% of each run, Pallas kernels for 0% -> 0%
where the time goes in v1:
time: 73.7 us; the launch traced here: 73.3 us
  waiting for transfers between devices  35.2 us (48%)
  between operations  18.6 us (25%)
  starting transfers between devices  12 us (16%)
  other arithmetic  5.56 us (8%)
  local copies, waits for them, and re-layouts  1.97 us (3%)
    reduce_scatter x1, waiting for transfers between devices, per_device(): mine = lax.psum_scatter(stacks, 'epoch', scatter_dimension=2, tiled=True)  22.9 us
    ppermute x4, waiting for transfers between devices, per_device(): from_left = lax.ppermute(from_left, 'vel', upward)  8.3 us
    ppermute x3, starting transfers between devices, per_device(): from_right = lax.ppermute(from_right, 'vel', left)  4.78 us
    ppermute x1, waiting for transfers between devices, extended(): lax.ppermute(lax.slice_in_dim(block, 0, width, axis=dim), axis, backward)  3.93 us
    ppermute x4, starting transfers between devices, per_device(): from_left = lax.ppermute(from_left, 'vel', upward)  3.55 us
    ppermute x1, starting transfers between devices, extended(): lax.ppermute(lax.slice_in_dim(block, block.shape[dim] - width, None, axis...  2.4 us
    another operation x2, other arithmetic, per_device(): weights = jnp.stack([psf, psf * psf], axis=1)  1.77 us
  transfers between devices with their start and end apart: 10, of which 5 were waited for; matrix products, arithmetic and copies ran while one was open for 1% of the time, Pallas kernels for 0%

profile of v1, /device:TPU:0, one launch (start us, length us, event | category | flops | bytes accessed | tf_op | source)
XLA Modules:
  0.0 73.3 jit_solution(3670587209043674819)
XLA Ops:
  6.5 0.7 multiply_bitcast_fusion
  7.2 1.1 %fusion.26 = (f32[2,2,1]{2,0,1:T(2,128)S(1)}, f32[2,2,1]{2,0,1:T(2,128)S(1)}, f32[2,2,1]{2,0,1:T(2,128)S(1)}, f32[2,2,1]{2,0,1:T(2,128)S(1)}, f32[2,2,1]{2,0,1:T...) fusion(f32[2,1,9]{2,0,1:T(2,128)} %bitcast.48, ...), kind=kLoop, calls=%fused_computation.75 | loop fusion | flops 36 | bytes 288 | tf_op jit(solution)/shard_map/stack | solution.py:49
  8.3 0.1 copy.11
  8.4 0.1 copy.12
  8.5 0.1 copy.13
  8.6 0.1 copy.5
  8.7 0.1 copy.6
  8.8 0.1 copy.7
  8.9 0.1 copy.8
  9.0 0.1 copy.9
  9.1 0.1 copy.10
  9.2 0.8 %divide_bitcast_fusion.1 = (f32[2,1,4,1024]{3,2,1,0:T(4,128)S(1)}, f32[2,1,4,1024]{3,2,1,0:T(4,128)S(1)}) fusion(f32[2,4,1024]{2,1,0:T(4,128)} %param.4, f32[2,4,1024]{2,1,0:T(4,128)} %param.5), kind=kLoop, calls=%fused_computation.45 | loop fusion | flops 16384 | bytes 131072 | tf_op jit(solution)/shard_map/stack | solution.py:48
  10.0 0.0 copy-start
  10.0 0.4 multiply_add_fusion
  10.4 2.4 %collective-permute-start = (f32[2,2,4,1024]{3,2,1,0:T(4,128)S(1)}, f32[2,2,4,1024]{3,2,1,0:T(4,128)S(1)}, u32[]{:S(2)}, u32[]{:S(2)}) collective-permute-start(f32[2,2,4,1024]{3,2,1,0:T(4,128)S(1)} %multiply_add_fusion), channel_id=1, source_target_pairs={{0,1},{1,2},{2,3},{3,4},{4,5},{5,6},{6,7},{8,9},{9,10},{10,11},{11... | collective-permute-start | bytes 196616 | tf_op jit(solution)/shard_map/ppermute | solution.py:14
  12.8 1.3 %collective-permute-start.1 = (f32[2,2,4,1024]{3,2,1,0:T(4,128)S(1)}, f32[2,2,4,1024]{3,2,1,0:T(4,128)S(1)}, u32[]{:S(2)}, u32[]{:S(2)}) collective-permute-start(f32[2,2,4,1024]{3,2,1,0:T(4,128)S(1)} %multiply_add_fusion), channel_id=1, source_target_pairs={{1,0},{2,1},{3,2},{4,3},{5,4},{6,5},{7,6},{9,8},{10,9},{11,10},{12... | collective-permute-start | bytes 196616 | tf_op jit(solution)/shard_map/ppermute | solution.py:17
  14.1 3.9 %collective-permute-done.1 = f32[2,2,4,1024]{3,2,1,0:T(4,128)S(1)} collective-permute-done((f32[2,2,4,1024]{3,2,1,0:T(4,128)S(1)}, f32[2,2,4,1024]{3,2,1,0:T(4,128)S(1)}, u32[]{:S(2)}, u32[]{:S(2)}) %collective-permute-start.1) | collective-permute-done | bytes 65568 | tf_op jit(solution)/shard_map/ppermute | solution.py:17
  18.1 0.3 constant_dynamic-update-slice_fusion.7
  18.4 3.0 %collective-permute-start.2 = (f32[2,2,4,1024]{3,2,1,0:T(4,128)S(1)}, f32[2,2,4,1024]{3,2,1,0:T(4,128)S(1)}, u32[]{:S(2)}, u32[]{:S(2)}) collective-permute-start(f32[2,2,4,1024]{3,2,1,0:T(4,128)S(1)} %get-tuple-element.28), channel_id=1, source_target_pairs={{0,1},{1,2},{2,3},{3,4},{4,5},{5,6},{6,7},{7,0},{8,9},{9,10},{10,1... | collective-permute-start | bytes 196616 | tf_op jit(solution)/shard_map/ppermute | solution.py:65
  21.4 0.0 collective-permute-start.3
  21.4 0.7 constant_dynamic-slice_fusion
  27.1 0.6 collective-permute-start.4
  27.7 2.1 %collective-permute-start.5 = (f32[2,2,4,1024]{3,2,1,0:T(4,128)S(1)}, f32[2,2,4,1024]{3,2,1,0:T(4,128)S(1)}, u32[]{:S(2)}, u32[]{:S(2)}) collective-permute-start(f32[2,2,4,1024]{3,2,1,0:T(4,128)S(1)} %collective-permute-done.3), channel_id=1, source_target_pairs={{0,7},{1,0},{2,1},{3,2},{4,3},{5,4},{6,5},{7,6},{8,15},{9,8},{10,9... | collective-permute-start | bytes 196616 | tf_op jit(solution)/shard_map/ppermute | solution.py:70
  29.9 1.9 %collective-permute-done.4 = f32[2,2,4,1024]{3,2,1,0:T(4,128)S(1)} collective-permute-done((f32[2,2,4,1024]{3,2,1,0:T(4,128)S(1)}, f32[2,2,4,1024]{3,2,1,0:T(4,128)S(1)}, u32[]{:S(2)}, u32[]{:S(2)}) %collective-permute-start.4) | collective-permute-done | bytes 65568 | tf_op jit(solution)/shard_map/ppermute | solution.py:65
  31.8 2.6 %collective-permute-start.7 = (f32[2,2,4,1024]{3,2,1,0:T(4,128)S(1)}, f32[2,2,4,1024]{3,2,1,0:T(4,128)S(1)}, u32[]{:S(2)}, u32[]{:S(2)}) collective-permute-start(f32[2,2,4,1024]{3,2,1,0:T(4,128)S(1)} %collective-permute-done.5), channel_id=1, source_target_pairs={{0,7},{1,0},{2,1},{3,2},{4,3},{5,4},{6,5},{7,6},{8,15},{9,8},{10,9... | collective-permute-start | bytes 196616 | tf_op jit(solution)/shard_map/ppermute | solution.py:70
  34.5 1.9 %collective-permute-done.6 = f32[2,2,4,1024]{3,2,1,0:T(4,128)S(1)} collective-permute-done((f32[2,2,4,1024]{3,2,1,0:T(4,128)S(1)}, f32[2,2,4,1024]{3,2,1,0:T(4,128)S(1)}, u32[]{:S(2)}, u32[]{:S(2)}) %collective-permute-start.6) | collective-permute-done | bytes 65568 | tf_op jit(solution)/shard_map/ppermute | solution.py:65
  36.4 4.5 %collective-permute-done.8 = f32[2,2,4,1024]{3,2,1,0:T(4,128)S(1)} collective-permute-done((f32[2,2,4,1024]{3,2,1,0:T(4,128)S(1)}, f32[2,2,4,1024]{3,2,1,0:T(4,128)S(1)}, u32[]{:S(2)}, u32[]{:S(2)}) %collective-permute-start.8) | collective-permute-done | bytes 65568 | tf_op jit(solution)/shard_map/ppermute | solution.py:65
  41.0 0.2 pad_slice_fusion.1
  41.2 0.9 %dynamic-slice_add_fusion = f32[1,2,32,1024]{3,2,1,0:T(8,128)} fusion(f32[1,2,64,1056]{3,2,1,0:T(8,128)S(1)} %get-tuple-element.30, s32[]{:T(128)} %bitcast.21, s32[]{:T(128)} %bitcast.24, f32[1,2,64,1056]{3,2,1,0:T(8,128)S(1)} %get-tuple-element.29, s32[]{:T(128)} %bitcast.15, s32[]{:T(128)} %bitcast.18), kind=kLoop, calls=%fused_computation.2 | loop fusion | flops 65536 | bytes 786448 | tf_op jit(solution)/shard_map/add | solution.py:85
  42.1 0.0 reduce-scatter.2.cloned.1.call-update
  42.1 22.9 %reduce-scatter.2.cloned.1.call-done = f32[1,2,8,1024]{3,2,1,0:T(8,128)} async-done(((f32[1,2,32,1024]{3,2,1,0:T(8,128)}), f32[1,2,8,1024]{3,2,1,0:T(8,128)}) %reduce-scatter.2.cloned.1.call-update) | async-done | bytes 65552 | tf_op jit(solution)/shard_map/reduce_scatter | solution.py:88
  65.1 1.4 %fusion.24 = f32[1,8,1024]{2,1,0:T(8,128)} fusion(f32[1,2,8,1024]{3,2,1,0:T(8,128)} %reduce-scatter.2.cloned.1.call-done), kind=kLoop, calls=%fused_computation.43 | loop fusion | flops 8192 | bytes 98304 | tf_op jit(solution)/shard_map/div | solution.py:89
  (18 shorter events, 0.2 us)
Async XLA Ops:
  6.5 58.5 %reduce-scatter.2.cloned.1.call-start = ((), (), s32[]{:S(2)}) async-start(), calls=%async_computation.1 | async-start | bytes 327680 | tf_op jit(solution)/shard_map/reduce_scatter | solution.py:88
  10.0 11.4 %copy-start = (s32[2,8,1]{1,2,0:T(1,128)S(1)}, s32[2,8,1]{1,2,0:T(1,128)}, u32[]{:S(2)}) copy-start(s32[2,8,1]{1,2,0:T(1,128)} %param.7) | copy-start | bytes 196
  10.4 3.7 %collective-permute-start = (f32[2,2,4,1024]{3,2,1,0:T(4,128)S(1)}, f32[2,2,4,1024]{3,2,1,0:T(4,128)S(1)}, u32[]{:S(2)}, u32[]{:S(2)}) collective-permute-start(f32[2,2,4,1024]{3,2,1,0:T(4,128)S(1)} %multiply_add_fusion), channel_id=1, source_target_pairs={{0,1},{1,2},{2,3},{3,4},{4,5},{5,6},{6,7},{8,9},{9,10},{10,11},{11... | collective-permute-start | bytes 196616 | tf_op jit(solution)/shard_map/ppermute | solution.py:14
  12.8 5.2 %collective-permute-start.1 = (f32[2,2,4,1024]{3,2,1,0:T(4,128)S(1)}, f32[2,2,4,1024]{3,2,1,0:T(4,128)S(1)}, u32[]{:S(2)}, u32[]{:S(2)}) collective-permute-start(f32[2,2,4,1024]{3,2,1,0:T(4,128)S(1)} %multiply_add_fusion), channel_id=1, source_target_pairs={{1,0},{2,1},{3,2},{4,3},{5,4},{6,5},{7,6},{9,8},{10,9},{11,10},{12... | collective-permute-start | bytes 196616 | tf_op jit(solution)/shard_map/ppermute | solution.py:17
  18.4 8.7 %collective-permute-start.2 = (f32[2,2,4,1024]{3,2,1,0:T(4,128)S(1)}, f32[2,2,4,1024]{3,2,1,0:T(4,128)S(1)}, u32[]{:S(2)}, u32[]{:S(2)}) collective-permute-start(f32[2,2,4,1024]{3,2,1,0:T(4,128)S(1)} %get-tuple-element.28), channel_id=1, source_target_pairs={{0,1},{1,2},{2,3},{3,4},{4,5},{5,6},{6,7},{7,0},{8,9},{9,10},{10,1... | collective-permute-start | bytes 196616 | tf_op jit(solution)/shard_map/ppermute | solution.py:65
  21.4 6.3 %collective-permute-start.3 = (f32[2,2,4,1024]{3,2,1,0:T(4,128)S(1)}, f32[2,2,4,1024]{3,2,1,0:T(4,128)S(1)}, u32[]{:S(2)}, u32[]{:S(2)}) collective-permute-start(f32[2,2,4,1024]{3,2,1,0:T(4,128)S(1)} %get-tuple-element.28), channel_id=1, source_target_pairs={{0,7},{1,0},{2,1},{3,2},{4,3},{5,4},{6,5},{7,6},{8,15},{9,8},{10,9... | collective-permute-start | bytes 196616 | tf_op jit(solution)/shard_map/ppermute | solution.py:70
  27.1 4.6 %collective-permute-start.4 = (f32[2,2,4,1024]{3,2,1,0:T(4,128)S(1)}, f32[2,2,4,1024]{3,2,1,0:T(4,128)S(1)}, u32[]{:S(2)}, u32[]{:S(2)}) collective-permute-start(f32[2,2,4,1024]{3,2,1,0:T(4,128)S(1)} %collective-permute-done.2), channel_id=1, source_target_pairs={{0,1},{1,2},{2,3},{3,4},{4,5},{5,6},{6,7},{7,0},{8,9},{9,10},{10,1... | collective-permute-start | bytes 196616 | tf_op jit(solution)/shard_map/ppermute | solution.py:65
  27.7 4.1 %collective-permute-start.5 = (f32[2,2,4,1024]{3,2,1,0:T(4,128)S(1)}, f32[2,2,4,1024]{3,2,1,0:T(4,128)S(1)}, u32[]{:S(2)}, u32[]{:S(2)}) collective-permute-start(f32[2,2,4,1024]{3,2,1,0:T(4,128)S(1)} %collective-permute-done.3), channel_id=1, source_target_pairs={{0,7},{1,0},{2,1},{3,2},{4,3},{5,4},{6,5},{7,6},{8,15},{9,8},{10,9... | collective-permute-start | bytes 196616 | tf_op jit(solution)/shard_map/ppermute | solution.py:70
  31.8 4.6 %collective-permute-start.6 = (f32[2,2,4,1024]{3,2,1,0:T(4,128)S(1)}, f32[2,2,4,1024]{3,2,1,0:T(4,128)S(1)}, u32[]{:S(2)}, u32[]{:S(2)}) collective-permute-start(f32[2,2,4,1024]{3,2,1,0:T(4,128)S(1)} %collective-permute-done.4), channel_id=1, source_target_pairs={{0,1},{1,2},{2,3},{3,4},{4,5},{5,6},{6,7},{7,0},{8,9},{9,10},{10,1... | collective-permute-start | bytes 196616 | tf_op jit(solution)/shard_map/ppermute | solution.py:65
  31.8 4.6 %collective-permute-start.7 = (f32[2,2,4,1024]{3,2,1,0:T(4,128)S(1)}, f32[2,2,4,1024]{3,2,1,0:T(4,128)S(1)}, u32[]{:S(2)}, u32[]{:S(2)}) collective-permute-start(f32[2,2,4,1024]{3,2,1,0:T(4,128)S(1)} %collective-permute-done.5), channel_id=1, source_target_pairs={{0,7},{1,0},{2,1},{3,2},{4,3},{5,4},{6,5},{7,6},{8,15},{9,8},{10,9... | collective-permute-start | bytes 196616 | tf_op jit(solution)/shard_map/ppermute | solution.py:70
  36.4 4.6 %collective-permute-start.8 = (f32[2,2,4,1024]{3,2,1,0:T(4,128)S(1)}, f32[2,2,4,1024]{3,2,1,0:T(4,128)S(1)}, u32[]{:S(2)}, u32[]{:S(2)}) collective-permute-start(f32[2,2,4,1024]{3,2,1,0:T(4,128)S(1)} %collective-permute-done.6), channel_id=1, source_target_pairs={{0,1},{1,2},{2,3},{3,4},{4,5},{5,6},{6,7},{7,0},{8,9},{9,10},{10,1... | collective-permute-start | bytes 196616 | tf_op jit(solution)/shard_map/ppermute | solution.py:65
Sparse Core Ops, SparseCore 0:
  42.3 22.7 reduce-scatter.1
